TPU v7x, 32 devices: a whole 2x2x4 slice. The times are simulated.
32 devices in a mesh: groups: 2 (over y), ctx: 8 (over z, x), head: 2 (over core).
Axes of the slice: x: 2, y: 2, z: 4, core: 2. Of those that a mesh axis runs over, the one named last changes fastest.
Arguments:
- queries: bfloat16 [2048, 2048], P(('groups', 'ctx'), 'head'), parts along dimension 0, may hold values from -16 to 16
- key_states: bfloat16 [2048, 1024], P(('groups', 'ctx'), 'head'), parts along dimension 0, may hold values from -16 to 16
- value_states: bfloat16 [2048, 1024], P(('groups', 'ctx'), 'head'), parts along dimension 0, may hold values from -6 to 6
- out_grad: bfloat16 [2048, 2048], P(('groups', 'ctx'), 'head'), parts along dimension 0, may hold values from -6 to 6
- doc_ids: int32 [32], P('groups'), parts along dimension 0, may hold values from 0 to 5, never falling along the last dimension, each value on 1 to 8 neighbouring positions
- int_pos: int32 [128], P('groups'), parts along dimension 0, may hold values from 0 to 127, as said below
- hidden: bfloat16 [128, 4608], P('groups', 'ctx'), parts along dimension 0, may hold values from -6 to 6
- upstream: bfloat16 [128, 4608], P('groups', 'ctx'), parts along dimension 0, may hold values from -3 to 3
- w_query: bfloat16 [4608, 2048], P('ctx', 'head'), may hold values from -0.09375 to 0.09375
- w_key: bfloat16 [4608, 1024], P('ctx', 'head'), may hold values from -0.09375 to 0.09375
- w_value: bfloat16 [4608, 1024], P('ctx', 'head'), may hold values from -0.09375 to 0.09375
- rotation: float32 [8, 4608], P(None, 'ctx'), may hold values from -0.09375 to 0.09375
- projection: float32 [8, 4608], P(None, 'ctx'), may hold values from -0.09375 to 0.09375
- rank_bias: float32 [8], replicated, may hold values from -4 to 4
Outputs:
- grad_rot: float32 [16, 4608], P('groups', 'ctx'), parts along dimension 0
- grad_proj: float32 [16, 4608], P('groups', 'ctx'), parts along dimension 0
- grad_bias: float32 [16], P('groups'), parts along dimension 0
There are 2 independent parts, one for each index of `groups`. A program takes and returns all parts, laid end to end along the dimension named above; an argument that names none is the same for every part. Nothing has to cross between parts.
Inputs may be any that keep to these rules, and one draw needn't show every extreme that they name: `doc_ids`: ids never fall along the blocks; each document covers 1 to 8 consecutive blocks, and one covers exactly 8. `int_pos`: each aligned group of 8 entries belongs to one block of 128 tokens and holds distinct token indices inside that block in rising order.
All inputs are finite; a program needn't handle non-finite values.
Results may differ from a plain program's by a relative error of at most 0.004.
The roundings to bfloat16 on the way count: a program that leaves them out, or rounds other values in their place, can miss the bound.
Values may be sent and summed in bfloat16 or wider, within the bound.
A program may use at most 64 MiB of HBM per device.

v0:
```python
import jax
import jax.numpy as jnp
from jax import lax
from jax.sharding import PartitionSpec as P

HD = 128
BLK = 64
POS_DEV = 8


scale_q = 1.0 / 12.0
soft_cap = 50.0
key_block = 512


def capping(dot_vals):
    return soft_cap * jnp.tanh(dot_vals * scale_q / soft_cap)


def doc_lookup(doc_table, block_idx):
    table_ids = jnp.arange(doc_table.shape[0], dtype=jnp.int32)
    return jnp.sum(
        jnp.where(block_idx[:, None] == table_ids[None, :], doc_table[None, :], 0), axis=1
    )


def local(
    queries,
    key_states,
    value_states,
    out_grad,
    doc_ids,
    int_pos,
    hidden,
    upstream,
    w_query,
    w_key,
    w_value,
    rotation,
    projection,
    rank_bias,
):
    tokens = queries.shape[0]
    kv_width = key_states.shape[1]
    groups_kv = kv_width // HD
    per_group = queries.shape[1] // kv_width
    pick_count = POS_DEV
    ctx_index = lax.axis_index("ctx")
    my_pos = lax.dynamic_slice_in_dim(int_pos, ctx_index * pick_count, pick_count, 0)
    query_pos = ctx_index * tokens + jnp.arange(tokens, dtype=jnp.int32)
    query_doc = doc_lookup(doc_ids, query_pos // BLK)
    pick_pos = ctx_index * tokens + my_pos
    pick_doc = doc_lookup(doc_ids, pick_pos // BLK)
    query_heads = queries.reshape(tokens, groups_kv, per_group, HD)
    grad_heads = out_grad.reshape(tokens, groups_kv, per_group, HD)
    pick_query = jnp.take(queries, my_pos, axis=0).reshape(pick_count, groups_kv, per_group, HD)
    pick_grad = jnp.take(out_grad, my_pos, axis=0).reshape(pick_count, groups_kv, per_group, HD)

    def visit_keys(running, kv_rows, first_row):
        z_total, numerator, main_sum, side_sum = running
        row_count = kv_rows.shape[0]
        key_pos = first_row + jnp.arange(row_count, dtype=jnp.int32)
        key_doc = doc_lookup(doc_ids, key_pos // BLK)
        key_heads = kv_rows[:, :kv_width].reshape(row_count, groups_kv, HD)
        value_heads = kv_rows[:, kv_width:].reshape(row_count, groups_kv, HD)
        capped = capping(
            jnp.einsum("tgqd,rgd->gqtr", query_heads, key_heads, preferred_element_type=jnp.float32)
        )
        visible = (
            (key_pos[None, :] <= query_pos[:, None])
            & (key_doc[None, :] == query_doc[:, None])
            & (key_pos[None, :] >= 0)
        )
        weights = jnp.where(visible, jnp.exp(capped), 0.0)
        z_total = z_total + jnp.sum(weights, axis=-1)
        numerator = numerator + jnp.einsum(
            "gqtr,rgd->tgqd",
            weights.astype(jnp.bfloat16),
            value_heads,
            preferred_element_type=jnp.float32,
        )
        pick_capped = capping(
            jnp.einsum("pgqd,rgd->gqpr", pick_query, key_heads, preferred_element_type=jnp.float32)
        )
        pick_visible = (
            (key_pos[None, :] <= pick_pos[:, None])
            & (key_doc[None, :] == pick_doc[:, None])
            & (key_pos[None, :] >= 0)
        )
        pick_weights = jnp.where(
            pick_visible, jnp.exp(pick_capped) * (1.0 - (pick_capped / soft_cap) ** 2), 0.0
        )
        prob_grad = jnp.einsum(
            "pgqd,rgd->gqpr", pick_grad, value_heads, preferred_element_type=jnp.float32
        )
        main_sum = main_sum + jnp.einsum(
            "gqpr,rgd->pgqd",
            (pick_weights * prob_grad).astype(jnp.bfloat16),
            key_heads,
            preferred_element_type=jnp.float32,
        )
        side_sum = side_sum + jnp.einsum(
            "gqpr,rgd->pgqd",
            pick_weights.astype(jnp.bfloat16),
            key_heads,
            preferred_element_type=jnp.float32,
        )
        return (z_total, numerator, main_sum, side_sum)

    kv_local = jnp.concatenate([key_states, value_states], axis=1)
    start_state = (
        jnp.zeros((groups_kv, per_group, tokens), jnp.float32),
        jnp.zeros((tokens, groups_kv, per_group, HD), jnp.float32),
        jnp.zeros((pick_count, groups_kv, per_group, HD), jnp.float32),
        jnp.zeros((pick_count, groups_kv, per_group, HD), jnp.float32),
    )
    running = start_state
    kv_piece = lax.all_gather(kv_local, "ctx", axis=0, tiled=True)
    row_count = kv_piece.shape[0]

    def one_block(accum_state, block_no):
        block_rows = lax.dynamic_slice_in_dim(kv_piece, block_no * key_block, key_block, 0)
        return (visit_keys(accum_state, block_rows, block_no * key_block), None)

    running, _ = lax.scan(one_block, running, jnp.arange(row_count // key_block, dtype=jnp.int32))
    z_total, numerator, main_sum, side_sum = running
    z_tok = jnp.transpose(z_total, (2, 0, 1))
    outputs = numerator / z_tok[..., None]
    row_delta = jnp.sum(grad_heads.astype(jnp.float32) * outputs, axis=-1)
    pick_z = jnp.take(z_tok, my_pos, axis=0)
    pick_delta = jnp.take(row_delta, my_pos, axis=0)
    dq_rows = (
        (scale_q * (main_sum - pick_delta[..., None] * side_sum) / pick_z[..., None])
        .reshape(pick_count, queries.shape[1])
        .astype(jnp.bfloat16)
    )
    delta_heads = jnp.transpose(row_delta, (1, 2, 0))
    picked = jnp.concatenate(
        [jnp.take(key_states, my_pos, axis=0), jnp.take(value_states, my_pos, axis=0)], axis=1
    )
    gathered = lax.all_gather(picked, "ctx", axis=0, tiled=True)
    block_rows = gathered
    row_ids = jnp.arange(pick_count * lax.axis_size("ctx"), dtype=jnp.int32)
    key_pos = row_ids // pick_count * tokens + int_pos
    row_count = block_rows.shape[0]
    key_doc = doc_lookup(doc_ids, key_pos // BLK)
    key_heads = block_rows[:, :kv_width].reshape(row_count, groups_kv, HD)
    value_heads = block_rows[:, kv_width:].reshape(row_count, groups_kv, HD)
    capped = capping(
        jnp.einsum("tgqd,rgd->gqtr", query_heads, key_heads, preferred_element_type=jnp.float32)
    )
    visible = (key_pos[None, :] <= query_pos[:, None]) & (key_doc[None, :] == query_doc[:, None])
    probs = jnp.where(visible, jnp.exp(capped), 0.0) / z_total[..., None]
    prob_grad = jnp.einsum(
        "tgqd,rgd->gqtr", grad_heads, value_heads, preferred_element_type=jnp.float32
    )
    dscore = probs * (prob_grad - delta_heads[..., None]) * (1.0 - (capped / soft_cap) ** 2)
    value_grad = jnp.einsum(
        "gqtr,tgqd->rgd", probs.astype(jnp.bfloat16), grad_heads, preferred_element_type=jnp.float32
    )
    key_grad = scale_q * jnp.einsum(
        "gqtr,tgqd->rgd",
        dscore.astype(jnp.bfloat16),
        query_heads,
        preferred_element_type=jnp.float32,
    )
    key_sums = lax.psum_scatter(
        jnp.concatenate(
            [key_grad.reshape(row_count, kv_width), value_grad.reshape(row_count, kv_width)], axis=1
        ),
        "ctx",
        scatter_dimension=0,
        tiled=True,
    )
    pos_rows = jnp.concatenate([dq_rows, key_sums.astype(jnp.bfloat16)], axis=1)
    weight_cat = jnp.concatenate([w_query, w_key, w_value], axis=1)
    partial_grad = lax.dot_general(
        lax.all_gather(pos_rows, "ctx", axis=0, tiled=True),
        weight_cat,
        (((1,), (1,)), ((), ())),
        preferred_element_type=jnp.float32,
    )
    resid_grad = lax.psum(partial_grad, "head") + upstream.astype(jnp.float32)
    hidden_wide = hidden.astype(jnp.float32)
    rank_part = jnp.dot(resid_grad, rotation.T, precision=lax.Precision.HIGHEST)
    state_part = jnp.dot(hidden_wide, (projection - rotation).T, precision=lax.Precision.HIGHEST)
    rank_grad, rank_state = lax.psum((rank_part, state_part), "ctx")
    rank_state = rank_state + rank_bias[None, :]
    grad_bias = jnp.sum(rank_grad, axis=0)
    grad_proj = jnp.dot(rank_grad.T, hidden_wide, precision=lax.Precision.HIGHEST)
    grad_rot = jnp.dot(rank_state.T, resid_grad, precision=lax.Precision.HIGHEST) - grad_proj
    return (grad_rot, grad_proj, grad_bias)


def solution(mesh):
    in_specs = (
        P(("groups", "ctx"), "head"),
        P(("groups", "ctx"), "head"),
        P(("groups", "ctx"), "head"),
        P(("groups", "ctx"), "head"),
        P("groups"),
        P("groups"),
        P("groups", "ctx"),
        P("groups", "ctx"),
        P("ctx", "head"),
        P("ctx", "head"),
        P("ctx", "head"),
        P(None, "ctx"),
        P(None, "ctx"),
        P(),
    )
    out_specs = (P("groups", "ctx"), P("groups", "ctx"), P("groups"))
    return jax.shard_map(local, mesh=mesh, in_specs=in_specs, out_specs=out_specs, check_vma=False)
```

profile of v0, /device:TPU:0, one launch (start us, length us, event | category | flops | bytes accessed | tf_op | source)
XLA Modules:
  0.0 219.9 jit_solution(13700051381468569167)
XLA Ops:
  7.3 1.1 copy.98
  8.4 1.0 copy.99
  9.4 0.7 pad_maximum_fusion
  10.3 1.1 copy.100
  11.4 0.7 compare_and_fusion.1
  12.1 1.6 gather_fusion
  13.7 0.6 gather_fusion.1
  14.3 0.2 copy.102
  14.5 0.6 gather_fusion.4
  15.1 0.6 gather_fusion.5
  15.6 0.2 copy.101
  15.9 32.5 %all_gather.10 = bf16[64,1024]{1,0:T(8,128)(2,1)S(1)} all-gather(bf16[8,1024]{1,0:T(8,128)(2,1)S(1)} %pad_maximum_fusion.3), channel_id=1, replica_groups=mesh['groups'=2,'ctx'=8,'head'=2] {'ctx'}, dimensions={0}, use_global_device_ids=true | all-gather | bytes 147456 | tf_op jit(solution)/shard_map/all_gather | solution.py:141
  48.5 0.1 and_select_fusion.2
  48.6 0.2 select_reduce_fusion.3
  48.8 0.1 select_reduce_fusion.2
  48.9 0.1 select_reduce_fusion.1
  49.0 0.1 compare_and_fusion
  49.1 0.1 broadcast_select_fusion
  49.2 0.2 fusion.22
  49.4 15.3 %all-gather.2.cloned.1.call-done = bf16[1024,1024]{0,1:T(8,128)(2,1)} async-done(((bf16[128,1024]{0,1:T(8,128)(2,1)}), bf16[1024,1024]{0,1:T(8,128)(2,1)}) %all-gather.2.cloned.1.call-update) | async-done | bytes 2097168 | tf_op jit(solution)/shard_map/all_gather | solution.py:118
  64.7 10.2 %while.20 = (s32[]{:T(128)}, f32[4,2,128]{2,1,0:T(2,128)S(1)}, f32[128,4,2,128]{0,3,2,1:T(8,128)S(1)}, f32[8,4,2,128]{3,0,2,1:T(8,128)S(1)}, f32[8,4,2,128]{3,0,...) while((s32[]{:T(128)}, f32[4,2,128]{2,1,0:T(2,128)S(1)}, ...), condition=%wide.region_6.8_spmd.clone, body=%wide.region_3.7_spmd.clone.sunk | while | flops 305514112 | bytes 9383324 | solution.py:125
  64.7 0.6 dynamic_slice.26
  65.9 0.1 select_reduce_fusion.5
  66.0 0.1 and_and_fusion.5
  66.1 1.3 fusion.113
  67.4 0.2 bitcast_select_fusion.4
  67.6 0.3 fusion.117
  67.9 0.3 and_and_fusion.4
  68.2 0.9 fusion.115
  69.1 0.4 fusion.116
  69.5 0.2 fusion.118
  69.8 0.6 dynamic_slice.26
  71.0 0.1 select_reduce_fusion.5
  71.1 0.1 and_and_fusion.5
  71.2 1.3 fusion.113
  72.5 0.2 bitcast_select_fusion.4
  72.7 0.3 fusion.117
  73.0 0.3 and_and_fusion.4
  73.3 0.9 fusion.115
  74.2 0.4 fusion.116
  74.6 0.2 fusion.118
  74.9 0.1 multiply_reduce_fusion
  75.0 0.2 convolution_bitcast_fusion.4
  75.2 0.3 fusion.28
  75.6 0.7 pad_maximum_fusion.1
  76.3 0.2 copy.105
  76.5 0.2 copy.103
  76.7 0.6 gather_fusion.2
  77.2 0.6 gather_fusion.3
  77.8 0.1 broadcast_select_fusion.3
  77.9 0.1 copy.106
  78.0 0.1 copy.107
  78.1 0.1 divide_convert_fusion
  78.2 57.9 %reduce-scatter.2.cloned.1.call-done = f32[8,1024]{1,0:T(8,128)} async-done(((f32[64,1024]{1,0:T(8,128)}), f32[8,1024]{1,0:T(8,128)}) %reduce-scatter.2.cloned.1.call-update) | async-done | bytes 32784 | tf_op jit(solution)/shard_map/reduce_scatter | solution.py:167
  136.1 0.8 convert_element_type.48
  136.8 30.9 %all_gather.11 = bf16[64,2048]{1,0:T(8,128)(2,1)S(1)} all-gather(bf16[8,2048]{1,0:T(8,128)(2,1)S(1)} %pad_maximum_fusion.2), channel_id=1, replica_groups=mesh['groups'=2,'ctx'=8,'head'=2] {'ctx'}, dimensions={0}, use_global_device_ids=true | all-gather | bytes 294912 | tf_op jit(solution)/shard_map/all_gather | solution.py:178
  167.8 2.8 %fusion.16 = f32[64,576]{1,0:T(8,128)} fusion(bf16[64,2048]{1,0:T(8,128)(2,1)S(1)} %all_gather.11, bf16[576,512]{1,0:T(8,128)(2,1)} %param.32, bf16[576,512]{1,0:T(8,128)(2,1)} %param.31, bf16[576,1024]{1,0:T(8,128)(2,1)S(1)} %copy-done.11), kind=kOutput, calls=%fused_computation.40 | convolution fusion | flops 158072832 | bytes 2768896 | tf_op jit(solution)/shard_map/dot_general | solution.py:177
  170.6 0.1 convolution_bitcast_fusion.6
  170.7 17.0 %all-reduce.3.cloned.1.call-done = f32[64,576]{1,0:T(8,128)} async-done(((f32[64,576]{1,0:T(8,128)}), f32[64,576]{1,0:T(8,128)}) %all-reduce.3.cloned.1.call-update) | async-done | bytes 147472 | tf_op jit(solution)/shard_map/psum | solution.py:183
  187.8 1.1 fusion.46
  188.9 21.9 %all-reduce = (f32[64,8]{0,1:T(8,128)S(1)}, f32[64,8]{0,1:T(8,128)S(1)}) all-reduce(f32[64,8]{0,1:T(8,128)S(1)} %fusion.46, f32[64,8]{0,1:T(8,128)S(1)} %convolution_bitcast_fusion.6), channel_id=1, replica_groups=mesh['groups'=2,'ctx'=8,'head'=2] {'ctx'}, use_global_device_ids=true, to_apply=%region_11.15 | all-reduce | flops 1024 | bytes 8192 | tf_op jit(solution)/shard_map/psum | solution.py:187
  210.8 0.1 fusion.65
  211.0 0.6 reduce_sum.75
  211.6 1.8 convolution_subtract_fusion
  (54 shorter events, 0.5 us)
Async XLA Ops:
  7.2 163.4 %copy-start = (bf16[64,576]{1,0:T(8,128)(2,1)S(1)}, bf16[64,576]{1,0:T(8,128)(2,1)}, u32[]{:S(2)}) copy-start(bf16[64,576]{1,0:T(8,128)(2,1)} %param.28) | copy-start | bytes 221188
  7.2 7.3 %copy-start.3 = (bf16[128,512]{1,0:T(8,128)(2,1)S(1)}, bf16[128,512]{1,0:T(8,128)(2,1)}, u32[]{:S(2)}) copy-start(bf16[128,512]{1,0:T(8,128)(2,1)} %param.23) | copy-start | bytes 393220
  7.2 7.9 %copy-start.4 = (bf16[128,512]{1,0:T(8,128)(2,1)S(1)}, bf16[128,512]{1,0:T(8,128)(2,1)}, u32[]{:S(2)}) copy-start(bf16[128,512]{1,0:T(8,128)(2,1)} %param.24) | copy-start | bytes 393220
  7.2 41.3 %copy-start.9 = (s32[64]{0:T(128)S(1)}, s32[64]{0:T(128)}, u32[]{:S(2)}) copy-start(s32[64]{0:T(128)} %param.27) | copy-start | bytes 772
  7.2 6.5 %copy-start.1 = (bf16[128,1024]{1,0:T(8,128)(2,1)S(1)}, bf16[128,1024]{1,0:T(8,128)(2,1)}, u32[]{:S(2)}) copy-start(bf16[128,1024]{1,0:T(8,128)(2,1)} %param.25) | copy-start | bytes 786436
  7.2 41.4 %copy-start.8 = (s32[16]{0:T(128)S(1)}, s32[16]{0:T(128)}, u32[]{:S(2)}) copy-start(s32[16]{0:T(128)} %param.26) | copy-start | bytes 196
  7.2 57.4 %all-gather.2.cloned.1.call-start = ((), (), s32[]{:S(2)}) async-start(), calls=%async_computation.1 | async-start | bytes 2359296 | tf_op jit(solution)/shard_map/all_gather | solution.py:118
  10.2 125.9 %reduce-scatter.2.cloned.1.call-start = ((), (), s32[]{:S(2)}) async-start(), calls=%async_computation.2 | async-start | bytes 294912 | tf_op jit(solution)/shard_map/reduce_scatter | solution.py:167
  75.2 92.6 %copy-start.11 = (bf16[576,1024]{1,0:T(8,128)(2,1)S(1)}, bf16[576,1024]{1,0:T(8,128)(2,1)}, u32[]{:S(2)}) copy-start(bf16[576,1024]{1,0:T(8,128)(2,1)} %param.30) | copy-start | bytes 3538948
  76.3 111.5 %all-reduce.3.cloned.1.call-start = ((), (), s32[]{:S(2)}) async-start(), calls=%async_computation.3 | async-start | bytes 327680 | tf_op jit(solution)/shard_map/psum | solution.py:183
  167.8 2.8 %copy-start.5 = (f32[8,576]{1,0:T(8,128)S(1)}, f32[8,576]{1,0:T(8,128)}, u32[]{:S(2)}) copy-start(f32[8,576]{1,0:T(8,128)} %param.33) | copy-start | bytes 55300
  167.8 2.9 %copy-start.7 = (f32[8,576]{1,0:T(8,128)S(1)}, f32[8,576]{1,0:T(8,128)}, u32[]{:S(2)}) copy-start(f32[8,576]{1,0:T(8,128)} %param.34) | copy-start | bytes 55300
  167.8 20.0 %copy-start.2 = (bf16[64,576]{1,0:T(8,128)(2,1)S(1)}, bf16[64,576]{1,0:T(8,128)(2,1)}, u32[]{:S(2)}) copy-start(bf16[64,576]{1,0:T(8,128)(2,1)} %param.29) | copy-start | bytes 221188
  167.8 43.8 %copy-start.10 = (f32[8]{0:T(128)S(1)}, f32[8]{0:T(128)}, u32[]{:S(2)}) copy-start(f32[8]{0:T(128)} %param.35) | copy-start | bytes 100
  211.0 2.4 %copy-start.6 = (f32[8,576]{1,0:T(8,128)}, f32[8,576]{1,0:T(8,128)S(1)}, u32[]{:S(2)}) copy-start(f32[8,576]{1,0:T(8,128)S(1)} %fusion.65) | copy-start | bytes 55300
Sparse Core Ops, SparseCore 0:
  10.3 54.3 all-gather.1
  76.4 59.6 reduce-scatter.1
  170.7 17.0 all-reduce.2
where the time goes:
time: 220 us
  waiting for transfers between devices  90.3 us (41%)
  blocking collectives  85.3 us (39%)
  between operations  14.1 us (6%)
  local copies, waits for them, and re-layouts  12.4 us (6%)
  matrix products  10.7 us (5%)
  other arithmetic  5.58 us (3%)
    reduce_scatter x1, waiting for transfers between devices, local(): lax.psum_scatter(jnp.concatenate([key_grad.reshape(row_count, kv_width),...  57.9 us
    all_gather x1, blocking collectives, local(): gathered = lax.all_gather(picked, 'ctx', axis=0, tiled=True)  32.5 us
    all_gather x1, blocking collectives, local(): lax.all_gather(pos_rows, 'ctx', axis=0, tiled=True)  30.9 us
    psum x1, blocking collectives, local(): rank_grad, rank_state = lax.psum((rank_part, state_part), 'ctx')  21.9 us
    psum x1, waiting for transfers between devices, local(): resid_grad = lax.psum(partial_grad, 'head') + upstream.astype(jnp.float32)  17 us
    all_gather x1, waiting for transfers between devices, local(): kv_piece = lax.all_gather(kv_local, 'ctx', axis=0, tiled=True)  15.3 us
  transfers between devices with their start and end apart: 3, of which 3 were waited for; matrix products, arithmetic and copies ran while one was open for 4% of the time, Pallas kernels for 0%

commit v1 on v0

v1 whole, which is shorter than its diff:
```python
import functools

import jax
import jax.numpy as jnp
from jax import lax
from jax.experimental import pallas as pl
from jax.experimental.pallas import tpu as pltpu
from jax.sharding import PartitionSpec as P

HD = 128
BLK = 64
POS_DEV = 8
LANES = 128

scale_q = 1.0 / 12.0
soft_cap = 50.0

MESH = pl.DeviceIdType.MESH
HIGHEST = lax.Precision.HIGHEST
F32 = jnp.float32
BF16 = jnp.bfloat16


def round_up(value, multiple):
    return (value + multiple - 1) // multiple * multiple


def dot_nt(left, right, precision=None):
    return lax.dot_general(
        left, right, (((1,), (1,)), ((), ())), preferred_element_type=F32, precision=precision
    )


def dot_tn(left, right):
    return lax.dot_general(left, right, (((0,), (0,)), ((), ())), preferred_element_type=F32)


def kernel(
    n,
    q_ref, k_ref, v_ref, g_ref, doc_ref, pos_ref, hidden_ref, up_ref,
    wq_hbm, wk_hbm, wv_hbm, rot_ref, proj_ref, bias_ref,
    rot_out, proj_out, bias_out,
    kbuf, vbuf, qa, ga, num, zs, ms, kp, vp, part, part_in, dq_rows, kv_rows,
    st_all, rg_all, gr_own, gr_in, wq, wk, wv,
    w_sem, ch_send, ch_recv, ex_send, ex_recv, st_send, st_recv, dq_send, dq_recv,
    pt_send, pt_recv, kv_send, kv_recv, rg_send, rg_recv, gr_send, gr_recv,
):
    me = lax.axis_index("ctx")
    core = lax.axis_index("head")
    odd = lax.rem(me, 2)
    partner = me + 1 - 2 * odd
    after = lax.rem(me + 2, n)
    halo = n // 2
    chain = halo // 2
    tokens = q_ref.shape[0]
    kv_width = k_ref.shape[1]
    heads = kv_width // HD
    positions = n * POS_DEV
    lanes = st_all.shape[2]
    width = hidden_ref.shape[1]
    rows = 2 * tokens + 2 * POS_DEV
    npick = kp.shape[0] * POS_DEV

    barrier = pltpu.get_barrier_semaphore()
    for k in range(1, n):
        for c in range(2):
            pl.semaphore_signal(
                barrier, inc=1, device_id={"ctx": lax.rem(me + k, n), "head": c},
                device_id_type=MESH,
            )
    pl.semaphore_signal(barrier, inc=1, device_id={"head": 1 - core}, device_id_type=MESH)

    loads = [
        pltpu.make_async_copy(src, dst, w_sem.at[i])
        for i, (src, dst) in enumerate(((wq_hbm, wq), (wk_hbm, wk), (wv_hbm, wv)))
    ]
    for load in loads:
        load.start()
    kbuf[0] = k_ref[...]
    vbuf[0] = v_ref[...]

    def send(src, dst, send_sem, recv_sem, **where):
        return pltpu.make_async_remote_copy(
            src_ref=src, dst_ref=dst, send_sem=send_sem, recv_sem=recv_sem,
            device_id=where, device_id_type=MESH,
        )

    bufs = (kbuf, vbuf)

    def chain_copy(j, p):
        return send(
            bufs[p].at[2 * j - 2], bufs[p].at[2 * j], ch_send.at[j - 1, p],
            ch_recv.at[j - 1, p], ctx=after,
        )

    def exchange_copy(j, p, to_slot, m):
        return send(
            bufs[p].at[2 * j], bufs[p].at[to_slot], ex_send.at[m, p], ex_recv.at[m, p],
            ctx=partner,
        )

    def exchange(j, run):
        if j < chain:
            @pl.when(odd == 0)
            def _():
                for p in range(2):
                    run(exchange_copy(j, p, 2 * j + 1, j))
        if j > 0:
            @pl.when(odd == 1)
            def _():
                for p in range(2):
                    run(exchange_copy(j, p, 2 * j - 1, j - 1))

    row8 = lax.broadcasted_iota(jnp.int32, (POS_DEV, LANES), 0)
    lane8 = lax.broadcasted_iota(jnp.int32, (POS_DEV, LANES), 1)

    def slot_pos(k):
        block = lax.rem(me - k + n, n)
        return [pos_ref[block * POS_DEV + r] for r in range(POS_DEV)]

    def column(values):
        out = jnp.zeros((POS_DEV, LANES), jnp.int32)
        for r in range(POS_DEV):
            out = jnp.where(row8 == r, values[r], out)
        return out

    def one_hot(values):
        return jnp.where(column(values) == lane8, 1.0, 0.0).astype(BF16)

    blocks = tokens // BLK
    starts = []
    for b in range(blocks):
        mine = doc_ref[me * blocks + b]
        starts.append(
            lax.fori_loop(
                0, doc_ref.shape[0],
                lambda i, s, mine=mine: s + jnp.where(doc_ref[i] < mine, BLK, 0),
                jnp.int32(0),
            )
        )

    def start_of(position):
        out = jnp.zeros(position.shape, jnp.int32) + starts[0]
        for b in range(1, blocks):
            out = jnp.where(position >= b * BLK, starts[b], out)
        return out

    mine = column(slot_pos(0))
    own = lax.broadcasted_iota(jnp.int32, (tokens, LANES), 0)
    local_pos = jnp.concatenate([own, own, mine, mine], axis=0)
    row_pos = local_pos + me * tokens
    row_start = start_of(local_pos)
    lane_all = lax.broadcasted_iota(jnp.int32, (rows, LANES), 1)

    pick = one_hot(slot_pos(0))
    q_pick = jnp.dot(pick, q_ref[...], preferred_element_type=F32)
    g_pick = jnp.dot(pick, g_ref[...], preferred_element_type=F32)
    for h in range(heads):
        a, b, c = 2 * h * HD, (2 * h + 1) * HD, (2 * h + 2) * HD
        for dst, src, picked in ((qa, q_ref, q_pick), (ga, g_ref, g_pick)):
            dst[h, :tokens] = src[:, a:b]
            dst[h, tokens : 2 * tokens] = src[:, b:c]
            dst[h, 2 * tokens :] = jnp.concatenate(
                [picked[:, a:b], picked[:, b:c]], axis=0
            ).astype(BF16)

    hidden_wide = hidden_ref[...].astype(F32)
    state = dot_nt(proj_ref[...] - rot_ref[...], hidden_wide, HIGHEST)
    if lanes > positions:
        st_all[me] = jnp.zeros(st_all.shape[1:], F32)
    st_all[me, :, :positions] = state

    pl.semaphore_wait(barrier, 2 * n - 1)

    for p in range(2):
        chain_copy(1, p).start()
    exchange(0, lambda copy: copy.start())

    def to_all(src, dst, send_sems, recv_sems):
        def copies():
            return [
                send(
                    src, dst.at[me], send_sems.at[k - 1], recv_sems.at[me],
                    ctx=lax.rem(me + k, n),
                )
                for k in range(1, n)
            ]

        def receives():
            return [
                send(
                    src, dst.at[lax.rem(me - k + n, n)], send_sems.at[k - 1],
                    recv_sems.at[lax.rem(me - k + n, n)], ctx=lax.rem(me + k, n),
                )
                for k in range(1, n)
            ]

        return copies, receives

    st_copies, st_receives = to_all(st_all.at[me], st_all, st_send, st_recv)
    for copy in st_copies():
        copy.start()

    if npick > (halo + 1) * POS_DEV:
        kp[halo + 1 :] = jnp.zeros((kp.shape[0] - halo - 1,) + kp.shape[1:], F32)
        vp[halo + 1 :] = jnp.zeros((vp.shape[0] - halo - 1,) + vp.shape[1:], F32)

    def visit(k):
        base = (me - k) * tokens
        key_pos = lane_all + base
        visible = (key_pos >= row_start) & (key_pos <= row_pos)
        hot = one_hot(slot_pos(k))
        kp[k] = jnp.dot(hot, kbuf[k], preferred_element_type=F32)
        vp[k] = jnp.dot(hot, vbuf[k], preferred_element_type=F32)
        for h in range(heads):
            cols = slice(h * HD, (h + 1) * HD)
            keys = kbuf[k, :, cols]
            values = vbuf[k, :, cols]
            bent = jnp.tanh(dot_nt(qa[h], keys) * (scale_q / soft_cap))
            weights = jnp.where(visible, jnp.exp(soft_cap * bent), 0.0)
            z_new = jnp.broadcast_to(jnp.sum(weights, axis=1, keepdims=True), (rows, LANES))
            num_new = jnp.dot(weights.astype(BF16), values, preferred_element_type=F32)
            bent_pick = bent[2 * tokens :]
            side = weights[2 * tokens :] * (1.0 - bent_pick * bent_pick)
            main = side * dot_nt(ga[h, 2 * tokens :], values)
            both = jnp.concatenate([main, side], axis=0).astype(BF16)
            ms_new = jnp.dot(both, keys, preferred_element_type=F32)
            if k == 0:
                zs[h], num[h], ms[h] = z_new, num_new, ms_new
            else:
                zs[h] += z_new
                num[h] += num_new
                ms[h] += ms_new

    visit(0)
    for j in range(1, chain + 1):
        for p in range(2):
            chain_copy(j, p).wait_recv()
            if j < chain:
                chain_copy(j + 1, p).start()
        exchange(j, lambda copy: copy.start())
        visit(2 * j)
        for p in range(2):
            send(
                bufs[p].at[0], bufs[p].at[2 * j - 1], ex_send.at[j - 1, p],
                ex_recv.at[j - 1, p], ctx=partner,
            ).wait_recv()
        visit(2 * j - 1)

    deltas = []
    for h in range(heads):
        inv = num[h] / zs[h]
        delta = jnp.sum(ga[h].astype(F32) * inv, axis=1, keepdims=True)
        deltas.append(delta)
        d_pick = delta[2 * tokens :]
        main, side = ms[h, : 2 * POS_DEV], ms[h, 2 * POS_DEV :]
        dq = scale_q * (main - d_pick * side) / zs[h, 2 * tokens :]
        for i in range(2):
            at = (2 * h + i) * HD
            dq_rows[me, :, at : at + HD] = dq[i * POS_DEV : (i + 1) * POS_DEV].astype(BF16)
    dq_copies, dq_receives = to_all(dq_rows.at[me], dq_rows, dq_send, dq_recv)
    for copy in dq_copies():
        copy.start()

    pick_lane = lax.broadcasted_iota(jnp.int32, (1, npick), 1)
    pick_pos = jnp.full((1, npick), -1, jnp.int32)
    for k in range(halo + 1):
        values = slot_pos(k)
        for r in range(POS_DEV):
            pick_pos = jnp.where(
                pick_lane == k * POS_DEV + r, (me - k) * tokens + values[r], pick_pos
            )
    seen = (pick_pos >= row_start[: 2 * tokens, :1]) & (pick_pos <= row_pos[: 2 * tokens, :1])
    for h in range(heads):
        cols = slice(h * HD, (h + 1) * HD)
        keys = kp[:, :, cols].reshape(npick, HD).astype(BF16)
        values = vp[:, :, cols].reshape(npick, HD).astype(BF16)
        query = qa[h, : 2 * tokens]
        grad = ga[h, : 2 * tokens]
        bent = jnp.tanh(dot_nt(query, keys) * (scale_q / soft_cap))
        prob = jnp.where(seen, jnp.exp(soft_cap * bent), 0.0) / zs[h, : 2 * tokens, :1]
        dscore = prob * (dot_nt(grad, values) - deltas[h][: 2 * tokens]) * (1.0 - bent * bent)
        dv = dot_tn(prob.astype(BF16), grad)
        dk = scale_q * dot_tn(dscore.astype(BF16), query)
        count = (halo + 1) * POS_DEV
        part[:, :, cols] = dk[:count].reshape(halo + 1, POS_DEV, HD)
        vcols = slice(kv_width + h * HD, kv_width + (h + 1) * HD)
        part[:, :, vcols] = dv[:count].reshape(halo + 1, POS_DEV, HD)

    def part_copy(k):
        return send(
            part.at[k], part_in.at[k - 1], pt_send.at[k - 1], pt_recv.at[k - 1],
            ctx=lax.rem(me - k + n, n),
        )

    for k in range(halo, 0, -1):
        part_copy(k).start()
    for load in loads:
        load.wait()
    for copy in dq_receives():
        copy.wait_recv()

    def all_rows(ref):
        return ref[...].astype(F32).reshape(positions, ref.shape[2]).astype(BF16)

    grad_part = dot_nt(all_rows(dq_rows), wq[...])
    grad_part = grad_part + jnp.where(core == 0, up_ref[...].astype(F32), 0.0)

    for copy in st_receives():
        copy.wait_recv()
    rank_state = st_all[0]
    for i in range(1, n):
        rank_state = rank_state + st_all[i]
    bias_row = lax.broadcasted_iota(jnp.int32, rank_state.shape, 0)
    for r in range(bias_ref.shape[0]):
        rank_state = rank_state + jnp.where(bias_row == r, bias_ref[r], 0.0)
    rank_state = rank_state[:, :positions]

    total = part[0]
    for k in range(1, halo + 1):
        part_copy(k).wait_recv()
        total = total + part_in[k - 1]
    kv_rows[me] = total.astype(BF16)
    kv_copies, kv_receives = to_all(kv_rows.at[me], kv_rows, kv_send, kv_recv)
    for copy in kv_copies():
        copy.start()
    for copy in kv_receives():
        copy.wait_recv()
    rows_kv = all_rows(kv_rows)
    grad_part = grad_part + dot_nt(rows_kv[:, :kv_width], wk[...])
    grad_part = grad_part + dot_nt(rows_kv[:, kv_width:], wv[...])

    my_slot = 2 * me + core
    if lanes > positions:
        rg_all[my_slot] = jnp.zeros(rg_all.shape[1:], F32)
    rg_all[my_slot, :, :positions] = dot_nt(rot_ref[...], grad_part, HIGHEST)

    def rank_copy(i, k, flip, receive):
        slot = my_slot
        other = jnp.where(flip == 1, 1 - core, core)
        if receive:
            slot = 2 * lax.rem(me - k + n, n) + other
        return send(
            rg_all.at[my_slot], rg_all.at[slot], rg_send.at[i], rg_recv.at[slot],
            ctx=lax.rem(me + k, n), head=other,
        )

    pairs = [(k, flip) for k in range(n) for flip in range(2) if k or flip]
    for i, (k, flip) in enumerate(pairs):
        rank_copy(i, k, flip, False).start()
    if gr_own.shape[1] > width:
        gr_own[...] = jnp.zeros(gr_own.shape, F32)
    gr_own[:, :width] = jnp.dot(
        rank_state, grad_part, precision=HIGHEST, preferred_element_type=F32
    )
    rot_copy = send(gr_own, gr_in, gr_send, gr_recv, head=1 - core)
    rot_copy.start()
    for i, (k, flip) in enumerate(pairs):
        rank_copy(i, k, flip, True).wait_recv()
    rank_grad = rg_all[0]
    for i in range(1, 2 * n):
        rank_grad = rank_grad + rg_all[i]
    rank_grad = rank_grad[:, :positions]
    grad_proj = jnp.dot(rank_grad, hidden_wide, precision=HIGHEST, preferred_element_type=F32)
    proj_out[...] = grad_proj
    bias_out[...] = jnp.sum(rank_grad, axis=1, keepdims=True)
    rot_copy.wait_recv()
    rot_out[...] = (gr_own[...] + gr_in[...])[:, :width] - grad_proj

    rot_copy.wait_send()
    for i, (k, flip) in enumerate(pairs):
        rank_copy(i, k, flip, False).wait_send()
    for copies in (st_copies, dq_copies, kv_copies):
        for copy in copies():
            copy.wait_send()
    for k in range(1, halo + 1):
        part_copy(k).wait_send()
    for j in range(1, chain + 1):
        for p in range(2):
            chain_copy(j, p).wait_send()
    for j in range(chain + 1):
        exchange(j, lambda copy: copy.wait_send())


def local(n, *args):
    queries, key_states = args[0], args[1]
    hidden, rotation = args[6], args[11]
    tokens, q_width = queries.shape
    kv_width = key_states.shape[1]
    heads = kv_width // HD
    width = hidden.shape[1]
    rank = rotation.shape[0]
    halo = n // 2
    chain = halo // 2
    positions = n * POS_DEV
    lanes = round_up(positions, LANES)
    wide = round_up(width, LANES)
    pick_slots = round_up((halo + 1) * POS_DEV, LANES) // POS_DEV
    rows = 2 * tokens + 2 * POS_DEV
    vmem = pl.BlockSpec(memory_space=pltpu.VMEM)
    smem = pl.BlockSpec(memory_space=pltpu.SMEM)
    hbm = pl.BlockSpec(memory_space=pl.ANY)
    dma = pltpu.SemaphoreType.DMA
    rot, proj, bias = pl.pallas_call(
        functools.partial(kernel, n),
        out_shape=(
            jax.ShapeDtypeStruct((rank, width), F32),
            jax.ShapeDtypeStruct((rank, width), F32),
            jax.ShapeDtypeStruct((rank, 1), F32),
        ),
        in_specs=[vmem] * 4 + [smem] * 2 + [vmem] * 2 + [hbm] * 3 + [vmem] * 2 + [smem],
        out_specs=(vmem, vmem, vmem),
        scratch_shapes=[
            pltpu.VMEM((halo + 1, tokens, kv_width), BF16),
            pltpu.VMEM((halo + 1, tokens, kv_width), BF16),
            pltpu.VMEM((heads, rows, HD), BF16),
            pltpu.VMEM((heads, rows, HD), BF16),
            pltpu.VMEM((heads, rows, HD), F32),
            pltpu.VMEM((heads, rows, LANES), F32),
            pltpu.VMEM((heads, 4 * POS_DEV, HD), F32),
            pltpu.VMEM((pick_slots, POS_DEV, kv_width), F32),
            pltpu.VMEM((pick_slots, POS_DEV, kv_width), F32),
            pltpu.VMEM((halo + 1, POS_DEV, 2 * kv_width), F32),
            pltpu.VMEM((halo, POS_DEV, 2 * kv_width), F32),
            pltpu.VMEM((n, POS_DEV, q_width), BF16),
            pltpu.VMEM((n, POS_DEV, 2 * kv_width), BF16),
            pltpu.VMEM((n, rank, lanes), F32),
            pltpu.VMEM((2 * n, rank, lanes), F32),
            pltpu.VMEM((rank, wide), F32),
            pltpu.VMEM((rank, wide), F32),
            pltpu.VMEM((width, q_width), BF16),
            pltpu.VMEM((width, kv_width), BF16),
            pltpu.VMEM((width, kv_width), BF16),
            dma((3,)),
            dma((chain, 2)), dma((chain, 2)),
            dma((chain, 2)), dma((chain, 2)),
            dma((n,)), dma((n,)),
            dma((n,)), dma((n,)),
            dma((halo,)), dma((halo,)),
            dma((n,)), dma((n,)),
            dma((2 * n,)), dma((2 * n,)),
            dma, dma,
        ],
        compiler_params=pltpu.CompilerParams(
            collective_id=0, has_side_effects=True, vmem_limit_bytes=52 << 20
        ),
        name="rank_backward",
    )(*args)
    return rot, proj, bias.reshape(rank)


def solution(mesh):
    in_specs = (
        P(("groups", "ctx"), "head"),
        P(("groups", "ctx"), "head"),
        P(("groups", "ctx"), "head"),
        P(("groups", "ctx"), "head"),
        P("groups"),
        P("groups"),
        P("groups", "ctx"),
        P("groups", "ctx"),
        P("ctx", "head"),
        P("ctx", "head"),
        P("ctx", "head"),
        P(None, "ctx"),
        P(None, "ctx"),
        P(),
    )
    out_specs = (P("groups", "ctx"), P("groups", "ctx"), P("groups"))
    return jax.shard_map(
        functools.partial(local, mesh.shape["ctx"]),
        mesh=mesh, in_specs=in_specs, out_specs=out_specs, check_vma=False,
    )
```

time: 220 us -> 62.2 us (0.28)
  waiting for transfers between devices: 90.3 us -> 0 us
  blocking collectives: 85.3 us -> 0 us
  Pallas kernels: 0 us -> 49.2 us
  between operations: 14.1 us -> 0.67 us
  matrix products: 10.7 us -> 0 us
  other arithmetic: 5.58 us -> 0.63 us
    all_gather x2 -> x0, blocking collectives: 63.4 us -> none  [the longest x1 32.5 us: local(): gathered = lax.all_gather(picked, 'ctx', axis=0, tiled=True)]
    reduce_scatter x1 -> x0, waiting for transfers between devices: 57.9 us -> none  [local(): lax.psum_scatter(jnp.concatenate([key_grad.reshape(row_count, kv_width),...]
    pallas_call x0 -> x1, Pallas kernels: none -> 49.2 us  [local(): pl.pallas_call(functools.partial(kernel, n), out_shape=(jax.ShapeDtypeStr...]
    psum x1 -> x0, blocking collectives: 21.9 us -> none  [local(): rank_grad, rank_state = lax.psum((rank_part, state_part), 'ctx')]
    psum x1 -> x0, waiting for transfers between devices: 17 us -> none  [local(): resid_grad = lax.psum(partial_grad, 'head') + upstream.astype(jnp.float32)]
    all_gather x1 -> x0, waiting for transfers between devices: 15.3 us -> none  [local(): kv_piece = lax.all_gather(kv_local, 'ctx', axis=0, tiled=True)]
    dot_general x18 -> x0, matrix products: 10.7 us -> none  [the longest x1 2.78 us: local(): lax.dot_general(lax.all_gather(pos_rows, 'ctx', axis=0, tiled=True), weig...]
    unnamed x29 -> x26, local copies, waits for them, and re-layouts: 3.66 us -> 11.2 us
  transfers between devices with their start and end apart: 3 -> 0, of which waited for: 3 -> 0; matrix products, arithmetic and copies ran while one was open for 4% -> 0% of each run, Pallas kernels for 0% -> 0%
where the time goes in v1:
time: 62.2 us; the launch traced here: 61.7 us
  Pallas kernels  49.2 us (79%)
  local copies, waits for them, and re-layouts  11.2 us (18%)
  between operations  0.67 us (1%)
  other arithmetic  0.63 us (1%)
    pallas_call x1, Pallas kernels, local(): pl.pallas_call(functools.partial(kernel, n), out_shape=(jax.ShapeDtypeStr...  49.2 us
    unnamed x26, local copies, waits for them, and re-layouts  11.2 us

profile of v1, /device:TPU:0, one launch (start us, length us, event | category | flops | bytes accessed | tf_op | source)
XLA Modules:
  0.0 61.7 jit_solution(9563371594900168264)
XLA Ops:
  0.6 0.0 copy-start
  0.6 1.1 %copy-done = bf16[576,512]{1,0:T(8,128)(2,1)S(1)} copy-done((bf16[576,512]{1,0:T(8,128)(2,1)S(1)}, bf16[576,512]{1,0:T(8,128)(2,1)}, u32[]{:S(2)}) %copy-start) | copy-done | bytes 589848
  1.7 0.0 copy-start.1
  1.7 0.9 %copy-done.1 = bf16[128,1024]{1,0:T(8,128)(2,1)S(1)} copy-done((bf16[128,1024]{1,0:T(8,128)(2,1)S(1)}, bf16[128,1024]{1,0:T(8,128)(2,1)}, u32[]{:S(2)}) %copy-start.1) | copy-done | bytes 262168
  2.7 0.0 copy-start.2
  2.7 0.9 %copy-done.2 = bf16[128,1024]{1,0:T(8,128)(2,1)S(1)} copy-done((bf16[128,1024]{1,0:T(8,128)(2,1)S(1)}, bf16[128,1024]{1,0:T(8,128)(2,1)}, u32[]{:S(2)}) %copy-start.2) | copy-done | bytes 262168
  3.6 0.0 copy-start.3
  3.6 0.9 %copy-done.3 = bf16[128,512]{1,0:T(8,128)(2,1)S(1)} copy-done((bf16[128,512]{1,0:T(8,128)(2,1)S(1)}, bf16[128,512]{1,0:T(8,128)(2,1)}, u32[]{:S(2)}) %copy-start.3) | copy-done | bytes 131096
  4.5 0.0 copy-start.4
  4.5 0.9 %copy-done.4 = bf16[128,512]{1,0:T(8,128)(2,1)S(1)} copy-done((bf16[128,512]{1,0:T(8,128)(2,1)S(1)}, bf16[128,512]{1,0:T(8,128)(2,1)}, u32[]{:S(2)}) %copy-start.4) | copy-done | bytes 131096
  5.4 0.0 copy-start.5
  5.4 0.9 %copy-done.5 = bf16[64,576]{1,0:T(8,128)(2,1)S(1)} copy-done((bf16[64,576]{1,0:T(8,128)(2,1)S(1)}, bf16[64,576]{1,0:T(8,128)(2,1)}, u32[]{:S(2)}) %copy-start.5) | copy-done | bytes 73752
  6.3 0.0 copy-start.6
  6.3 0.9 %copy-done.6 = bf16[64,576]{1,0:T(8,128)(2,1)S(1)} copy-done((bf16[64,576]{1,0:T(8,128)(2,1)S(1)}, bf16[64,576]{1,0:T(8,128)(2,1)}, u32[]{:S(2)}) %copy-start.6) | copy-done | bytes 73752
  7.2 0.0 copy-start.7
  7.2 0.7 %copy-done.7 = f32[8,576]{1,0:T(8,128)S(1)} copy-done((f32[8,576]{1,0:T(8,128)S(1)}, f32[8,576]{1,0:T(8,128)}, u32[]{:S(2)}) %copy-start.7) | copy-done | bytes 18456
  7.9 0.0 copy-start.8
  7.9 0.7 %copy-done.8 = f32[8,576]{1,0:T(8,128)S(1)} copy-done((f32[8,576]{1,0:T(8,128)S(1)}, f32[8,576]{1,0:T(8,128)}, u32[]{:S(2)}) %copy-start.8) | copy-done | bytes 18456
  8.6 0.0 copy-start.9
  8.6 0.7 %copy-done.9 = s32[16]{0:T(128)S(1)} copy-done((s32[16]{0:T(128)S(1)}, s32[16]{0:T(128)}, u32[]{:S(2)}) %copy-start.9) | copy-done | bytes 88
  9.3 0.0 copy-start.10
  9.3 0.7 %copy-done.10 = s32[64]{0:T(128)S(1)} copy-done((s32[64]{0:T(128)S(1)}, s32[64]{0:T(128)}, u32[]{:S(2)}) %copy-start.10) | copy-done | bytes 280
  10.0 0.0 copy-start.11
  10.0 0.7 %copy-done.11 = f32[8]{0:T(128)S(1)} copy-done((f32[8]{0:T(128)S(1)}, f32[8]{0:T(128)}, u32[]{:S(2)}) %copy-start.11) | copy-done | bytes 56
  10.6 49.2 %rank_backward.1 = (f32[8,576]{1,0:T(8,128)S(1)}, f32[8,576]{1,0:T(8,128)S(1)}, f32[8,1]{1,0:T(8,128)S(1)}) custom-call(bf16[128,1024]{1,0:T(8,128)(2,1)S(1)} %copy-done.1, bf16[128,512]{1,0:T(8,128)(2,1)S(1)} %copy-done.3, bf16[128,512]{1,0:T(8,128)(2,1)S(1)} %copy-done.4, bf16[128,1024]{1,0:T(8,128)(2,1)S(1)} %copy-done.2, s32[16]{0:T(128)S(1)} %copy-done.9, ...), custom_call_target="tpu_custom_call" | custom-call | tf_op jit(solution)/shard_map/rank_backward/pallas_call | solution.py:404
  59.8 0.6 %reduce = f32[8]{0:T(128)} reduce(f32[8,1]{1,0:T(8,128)S(1)} %get-tuple-element.8, f32[]{:T(128)} %constant), dimensions={1}, to_apply=%get-tuple-element.8.reduce_sub_computation | reduce | bytes 68 | tf_op jit(solution)/shard_map/rank_backward/pallas_call | solution.py:404
  60.5 0.6 copy.19
  61.1 0.6 copy.20
Async XLA Ops:
  0.6 1.1 %copy-start = (bf16[576,512]{1,0:T(8,128)(2,1)S(1)}, bf16[576,512]{1,0:T(8,128)(2,1)}, u32[]{:S(2)}) copy-start(bf16[576,512]{1,0:T(8,128)(2,1)} %wk_hbm.1) | copy-start | bytes 1769476
  1.7 0.9 %copy-start.1 = (bf16[128,1024]{1,0:T(8,128)(2,1)S(1)}, bf16[128,1024]{1,0:T(8,128)(2,1)}, u32[]{:S(2)}) copy-start(bf16[128,1024]{1,0:T(8,128)(2,1)} %q_ref.1) | copy-start | bytes 786436
  2.7 0.9 %copy-start.2 = (bf16[128,1024]{1,0:T(8,128)(2,1)S(1)}, bf16[128,1024]{1,0:T(8,128)(2,1)}, u32[]{:S(2)}) copy-start(bf16[128,1024]{1,0:T(8,128)(2,1)} %g_ref.1) | copy-start | bytes 786436
  3.6 0.9 %copy-start.3 = (bf16[128,512]{1,0:T(8,128)(2,1)S(1)}, bf16[128,512]{1,0:T(8,128)(2,1)}, u32[]{:S(2)}) copy-start(bf16[128,512]{1,0:T(8,128)(2,1)} %k_ref.1) | copy-start | bytes 393220
  4.5 0.9 %copy-start.4 = (bf16[128,512]{1,0:T(8,128)(2,1)S(1)}, bf16[128,512]{1,0:T(8,128)(2,1)}, u32[]{:S(2)}) copy-start(bf16[128,512]{1,0:T(8,128)(2,1)} %v_ref.1) | copy-start | bytes 393220
  5.4 0.9 %copy-start.5 = (bf16[64,576]{1,0:T(8,128)(2,1)S(1)}, bf16[64,576]{1,0:T(8,128)(2,1)}, u32[]{:S(2)}) copy-start(bf16[64,576]{1,0:T(8,128)(2,1)} %hidden_ref.1) | copy-start | bytes 221188
  6.3 0.9 %copy-start.6 = (bf16[64,576]{1,0:T(8,128)(2,1)S(1)}, bf16[64,576]{1,0:T(8,128)(2,1)}, u32[]{:S(2)}) copy-start(bf16[64,576]{1,0:T(8,128)(2,1)} %up_ref.1) | copy-start | bytes 221188
  7.2 0.7 %copy-start.7 = (f32[8,576]{1,0:T(8,128)S(1)}, f32[8,576]{1,0:T(8,128)}, u32[]{:S(2)}) copy-start(f32[8,576]{1,0:T(8,128)} %rot_ref.1) | copy-start | bytes 55300
  7.9 0.7 %copy-start.8 = (f32[8,576]{1,0:T(8,128)S(1)}, f32[8,576]{1,0:T(8,128)}, u32[]{:S(2)}) copy-start(f32[8,576]{1,0:T(8,128)} %proj_ref.1) | copy-start | bytes 55300
  8.6 0.7 %copy-start.9 = (s32[16]{0:T(128)S(1)}, s32[16]{0:T(128)}, u32[]{:S(2)}) copy-start(s32[16]{0:T(128)} %doc_ref.1) | copy-start | bytes 196
  9.3 0.7 %copy-start.10 = (s32[64]{0:T(128)S(1)}, s32[64]{0:T(128)}, u32[]{:S(2)}) copy-start(s32[64]{0:T(128)} %pos_ref.1) | copy-start | bytes 772
  10.0 0.7 %copy-start.11 = (f32[8]{0:T(128)S(1)}, f32[8]{0:T(128)}, u32[]{:S(2)}) copy-start(f32[8]{0:T(128)} %bias_ref.1) | copy-start | bytes 100

commit v2 on v1

--- a/solution.py
+++ b/solution.py
@@ -37,11 +37,12 @@
 
 def kernel(
     n,
-    q_ref, k_ref, v_ref, g_ref, doc_ref, pos_ref, hidden_ref, up_ref,
-    wq_hbm, wk_hbm, wv_hbm, rot_ref, proj_ref, bias_ref,
+    q_hbm, k_hbm, v_hbm, g_hbm, doc_hbm, pos_hbm, hidden_hbm, up_hbm,
+    wq_hbm, wk_hbm, wv_hbm, rot_hbm, proj_hbm, bias_hbm,
     rot_out, proj_out, bias_out,
     kbuf, vbuf, qa, ga, num, zs, ms, kp, vp, part, part_in, dq_rows, kv_rows,
     st_all, rg_all, gr_own, gr_in, wq, wk, wv,
+    q_ref, g_ref, doc_ref, pos_ref, hidden_ref, up_ref, rot_ref, proj_ref, bias_ref,
     w_sem, ch_send, ch_recv, ex_send, ex_recv, st_send, st_recv, dq_send, dq_recv,
     pt_send, pt_recv, kv_send, kv_recv, rg_send, rg_recv, gr_send, gr_recv,
 ):
@@ -53,7 +54,7 @@
     halo = n // 2
     chain = halo // 2
     tokens = q_ref.shape[0]
-    kv_width = k_ref.shape[1]
+    kv_width = kbuf.shape[2]
     heads = kv_width // HD
     positions = n * POS_DEV
     lanes = st_all.shape[2]
@@ -70,14 +71,17 @@
             )
     pl.semaphore_signal(barrier, inc=1, device_id={"head": 1 - core}, device_id_type=MESH)
 
+    pairs_in = (
+        (k_hbm, kbuf.at[0]), (v_hbm, vbuf.at[0]), (doc_hbm, doc_ref), (pos_hbm, pos_ref),
+        (q_hbm, q_ref), (g_hbm, g_ref), (rot_hbm, rot_ref), (proj_hbm, proj_ref),
+        (hidden_hbm, hidden_ref), (bias_hbm, bias_ref), (up_hbm, up_ref),
+        (wq_hbm, wq), (wk_hbm, wk), (wv_hbm, wv),
+    )
     loads = [
-        pltpu.make_async_copy(src, dst, w_sem.at[i])
-        for i, (src, dst) in enumerate(((wq_hbm, wq), (wk_hbm, wk), (wv_hbm, wv)))
+        pltpu.make_async_copy(src, dst, w_sem.at[i]) for i, (src, dst) in enumerate(pairs_in)
     ]
     for load in loads:
         load.start()
-    kbuf[0] = k_ref[...]
-    vbuf[0] = v_ref[...]
 
     def send(src, dst, send_sem, recv_sem, **where):
         return pltpu.make_async_remote_copy(
@@ -111,8 +115,19 @@
                 for p in range(2):
                     run(exchange_copy(j, p, 2 * j - 1, j - 1))
 
+    loads[0].wait()
+    loads[1].wait()
+    pl.semaphore_wait(barrier, 2 * n - 1)
+
+    for p in range(2):
+        chain_copy(1, p).start()
+    exchange(0, lambda copy: copy.start())
+
     row8 = lax.broadcasted_iota(jnp.int32, (POS_DEV, LANES), 0)
     lane8 = lax.broadcasted_iota(jnp.int32, (POS_DEV, LANES), 1)
+
+    for load in loads[2:10]:
+        load.wait()
 
     def slot_pos(k):
         block = lax.rem(me - k + n, n)
@@ -169,12 +184,6 @@
     if lanes > positions:
         st_all[me] = jnp.zeros(st_all.shape[1:], F32)
     st_all[me, :, :positions] = state
-
-    pl.semaphore_wait(barrier, 2 * n - 1)
-
-    for p in range(2):
-        chain_copy(1, p).start()
-    exchange(0, lambda copy: copy.start())
 
     def to_all(src, dst, send_sems, recv_sems):
         def copies():
@@ -218,7 +227,6 @@
             values = vbuf[k, :, cols]
             bent = jnp.tanh(dot_nt(qa[h], keys) * (scale_q / soft_cap))
             weights = jnp.where(visible, jnp.exp(soft_cap * bent), 0.0)
-            z_new = jnp.broadcast_to(jnp.sum(weights, axis=1, keepdims=True), (rows, LANES))
             num_new = jnp.dot(weights.astype(BF16), values, preferred_element_type=F32)
             bent_pick = bent[2 * tokens :]
             side = weights[2 * tokens :] * (1.0 - bent_pick * bent_pick)
@@ -226,9 +234,9 @@
             both = jnp.concatenate([main, side], axis=0).astype(BF16)
             ms_new = jnp.dot(both, keys, preferred_element_type=F32)
             if k == 0:
-                zs[h], num[h], ms[h] = z_new, num_new, ms_new
+                zs[h], num[h], ms[h] = weights, num_new, ms_new
             else:
-                zs[h] += z_new
+                zs[h] += weights
                 num[h] += num_new
                 ms[h] += ms_new
 
@@ -249,7 +257,9 @@
 
     deltas = []
     for h in range(heads):
-        inv = num[h] / zs[h]
+        total = jnp.sum(zs[h], axis=1, keepdims=True)
+        zs[h] = jnp.broadcast_to(total, (rows, LANES))
+        inv = num[h] / total
         delta = jnp.sum(ga[h].astype(F32) * inv, axis=1, keepdims=True)
         deltas.append(delta)
         d_pick = delta[2 * tokens :]
@@ -295,7 +305,7 @@
 
     for k in range(halo, 0, -1):
         part_copy(k).start()
-    for load in loads:
+    for load in loads[10:]:
         load.wait()
     for copy in dq_receives():
         copy.wait_recv()
@@ -363,7 +373,8 @@
     rank_grad = rank_grad[:, :positions]
     grad_proj = jnp.dot(rank_grad, hidden_wide, precision=HIGHEST, preferred_element_type=F32)
     proj_out[...] = grad_proj
-    bias_out[...] = jnp.sum(rank_grad, axis=1, keepdims=True)
+    for r in range(bias_out.shape[0]):
+        bias_out[r] = jnp.sum(rank_grad[r : r + 1])
     rot_copy.wait_recv()
     rot_out[...] = (gr_own[...] + gr_in[...])[:, :width] - grad_proj
 
@@ -399,17 +410,17 @@
     rows = 2 * tokens + 2 * POS_DEV
     vmem = pl.BlockSpec(memory_space=pltpu.VMEM)
     smem = pl.BlockSpec(memory_space=pltpu.SMEM)
-    hbm = pl.BlockSpec(memory_space=pl.ANY)
+    hbm = pl.BlockSpec(memory_space=pltpu.HBM)
     dma = pltpu.SemaphoreType.DMA
     rot, proj, bias = pl.pallas_call(
         functools.partial(kernel, n),
         out_shape=(
             jax.ShapeDtypeStruct((rank, width), F32),
             jax.ShapeDtypeStruct((rank, width), F32),
-            jax.ShapeDtypeStruct((rank, 1), F32),
+            jax.ShapeDtypeStruct((rank,), F32),
         ),
-        in_specs=[vmem] * 4 + [smem] * 2 + [vmem] * 2 + [hbm] * 3 + [vmem] * 2 + [smem],
-        out_specs=(vmem, vmem, vmem),
+        in_specs=[hbm] * len(args),
+        out_specs=(vmem, vmem, smem),
         scratch_shapes=[
             pltpu.VMEM((halo + 1, tokens, kv_width), BF16),
             pltpu.VMEM((halo + 1, tokens, kv_width), BF16),
@@ -431,7 +442,16 @@
             pltpu.VMEM((width, q_width), BF16),
             pltpu.VMEM((width, kv_width), BF16),
             pltpu.VMEM((width, kv_width), BF16),
-            dma((3,)),
+            pltpu.VMEM((tokens, q_width), BF16),
+            pltpu.VMEM((tokens, q_width), BF16),
+            pltpu.SMEM(args[4].shape, jnp.int32),
+            pltpu.SMEM(args[5].shape, jnp.int32),
+            pltpu.VMEM(hidden.shape, BF16),
+            pltpu.VMEM(hidden.shape, BF16),
+            pltpu.VMEM(rotation.shape, F32),
+            pltpu.VMEM(rotation.shape, F32),
+            pltpu.SMEM((rank,), F32),
+            dma((len(args),)),
             dma((chain, 2)), dma((chain, 2)),
             dma((chain, 2)), dma((chain, 2)),
             dma((n,)), dma((n,)),
@@ -442,11 +462,11 @@
             dma, dma,
         ],
         compiler_params=pltpu.CompilerParams(
-            collective_id=0, has_side_effects=True, vmem_limit_bytes=52 << 20
+            collective_id=0, has_side_effects=True, vmem_limit_bytes=64 << 20
         ),
         name="rank_backward",
     )(*args)
-    return rot, proj, bias.reshape(rank)
+    return rot, proj, bias
 
 
 def solution(mesh):

time: 62.2 us -> 54.1 us (0.87)
  local copies, waits for them, and re-layouts: 11.2 us -> 3.79 us
  other arithmetic: 0.63 us -> 0 us
    unnamed x26 -> x3, local copies, waits for them, and re-layouts: 11.2 us -> 3.79 us
    pallas_call x1 -> x0, other arithmetic: 0.63 us -> none  [local(): pl.pallas_call(functools.partial(kernel, n), out_shape=(jax.ShapeDtypeStr...]
where the time goes in v2:
time: 54.1 us; the launch traced here: 53.9 us
  Pallas kernels  49.5 us (91%)
  local copies, waits for them, and re-layouts  3.79 us (7%)
  between operations  0.65 us (1%)
    pallas_call x1, Pallas kernels, local(): pl.pallas_call(functools.partial(kernel, n), out_shape=(jax.ShapeDtypeStr...  49.5 us
    unnamed x3, local copies, waits for them, and re-layouts  3.79 us

profile of v2, /device:TPU:0, one launch (start us, length us, event | category | flops | bytes accessed | tf_op | source)
XLA Modules:
  0.0 53.9 jit_solution(9414383864839319942)
XLA Ops:
  0.6 49.5 %rank_backward.1 = (f32[8,576]{1,0:T(8,128)}, f32[8,576]{1,0:T(8,128)}, f32[8]{0:T(128)}) custom-call(bf16[128,1024]{1,0:T(8,128)(2,1)} %q_hbm.1, bf16[128,512]{1,0:T(8,128)(2,1)} %k_hbm.1, bf16[128,512]{1,0:T(8,128)(2,1)} %v_hbm.1, bf16[128,1024]{1,0:T(8,128)(2,1)} %g_hbm.1, s32[16]{0:T(128)} %doc_hbm.1, s32[64]{0:T(128)} %pos_hbm.1, ...), custom_call_target="tpu_custom_call" | custom-call | tf_op jit(solution)/shard_map/rank_backward/pallas_call | solution.py:415
  50.1 1.3 %copy.20 = f32[8,576]{1,0:T(8,128)} copy(f32[8,576]{1,0:T(8,128)} %get-tuple-element.6) | data formatting | bytes 36864
  51.4 1.3 %copy.21 = f32[8,576]{1,0:T(8,128)} copy(f32[8,576]{1,0:T(8,128)} %get-tuple-element.7) | data formatting | bytes 36864
  52.8 1.1 %copy.22 = f32[8]{0:T(128)} copy(f32[8]{0:T(128)} %get-tuple-element.8) | data formatting | bytes 64

commit v3 on v2

--- a/solution.py
+++ b/solution.py
@@ -11,6 +11,7 @@
 BLK = 64
 POS_DEV = 8
 LANES = 128
+PIECES = 4
 
 scale_q = 1.0 / 12.0
 soft_cap = 50.0
@@ -89,39 +90,40 @@
             device_id=where, device_id_type=MESH,
         )
 
-    bufs = (kbuf, vbuf)
+    half = tokens // 2
+
+    def piece(p, slot):
+        return (kbuf, vbuf)[p // 2].at[slot, pl.ds(p % 2 * half, half)]
 
     def chain_copy(j, p):
         return send(
-            bufs[p].at[2 * j - 2], bufs[p].at[2 * j], ch_send.at[j - 1, p],
+            piece(p, 2 * j - 2), piece(p, 2 * j), ch_send.at[j - 1, p],
             ch_recv.at[j - 1, p], ctx=after,
         )
 
     def exchange_copy(j, p, to_slot, m):
         return send(
-            bufs[p].at[2 * j], bufs[p].at[to_slot], ex_send.at[m, p], ex_recv.at[m, p],
+            piece(p, 2 * j), piece(p, to_slot), ex_send.at[m, p], ex_recv.at[m, p],
             ctx=partner,
         )
 
-    def exchange(j, run):
+    def exchange(j, p, run):
         if j < chain:
             @pl.when(odd == 0)
             def _():
-                for p in range(2):
-                    run(exchange_copy(j, p, 2 * j + 1, j))
+                run(exchange_copy(j, p, 2 * j + 1, j))
         if j > 0:
             @pl.when(odd == 1)
             def _():
-                for p in range(2):
-                    run(exchange_copy(j, p, 2 * j - 1, j - 1))
+                run(exchange_copy(j, p, 2 * j - 1, j - 1))
 
     loads[0].wait()
     loads[1].wait()
     pl.semaphore_wait(barrier, 2 * n - 1)
 
-    for p in range(2):
+    for p in range(PIECES):
         chain_copy(1, p).start()
-    exchange(0, lambda copy: copy.start())
+        exchange(0, p, lambda copy: copy.start())
 
     row8 = lax.broadcasted_iota(jnp.int32, (POS_DEV, LANES), 0)
     lane8 = lax.broadcasted_iota(jnp.int32, (POS_DEV, LANES), 1)
@@ -242,15 +244,29 @@
 
     visit(0)
     for j in range(1, chain + 1):
-        for p in range(2):
+        for p in range(PIECES):
             chain_copy(j, p).wait_recv()
             if j < chain:
                 chain_copy(j + 1, p).start()
-        exchange(j, lambda copy: copy.start())
+            exchange(j, p, lambda copy: copy.start())
         visit(2 * j)
-        for p in range(2):
+        if j == 1:
+            for copy in st_receives():
+                copy.wait_recv()
+            rank_state = st_all[0]
+            for i in range(1, n):
+                rank_state = rank_state + st_all[i]
+            bias_row = lax.broadcasted_iota(jnp.int32, rank_state.shape, 0)
+            for r in range(bias_ref.shape[0]):
+                rank_state = rank_state + jnp.where(bias_row == r, bias_ref[r], 0.0)
+            rank_state = rank_state[:, :positions]
+            loads[10].wait()
+            up = jnp.where(core == 0, up_ref[...].astype(F32), 0.0)
+            rank_up = dot_nt(rot_ref[...], up, HIGHEST)
+            rot_up = jnp.dot(rank_state, up, precision=HIGHEST, preferred_element_type=F32)
+        for p in range(PIECES):
             send(
-                bufs[p].at[0], bufs[p].at[2 * j - 1], ex_send.at[j - 1, p],
+                piece(p, 0), piece(p, 2 * j - 1), ex_send.at[j - 1, p],
                 ex_recv.at[j - 1, p], ctx=partner,
             ).wait_recv()
         visit(2 * j - 1)
@@ -305,7 +321,7 @@
 
     for k in range(halo, 0, -1):
         part_copy(k).start()
-    for load in loads[10:]:
+    for load in loads[11:]:
         load.wait()
     for copy in dq_receives():
         copy.wait_recv()
@@ -313,18 +329,7 @@
     def all_rows(ref):
         return ref[...].astype(F32).reshape(positions, ref.shape[2]).astype(BF16)
 
-    grad_part = dot_nt(all_rows(dq_rows), wq[...])
-    grad_part = grad_part + jnp.where(core == 0, up_ref[...].astype(F32), 0.0)
-
-    for copy in st_receives():
-        copy.wait_recv()
-    rank_state = st_all[0]
-    for i in range(1, n):
-        rank_state = rank_state + st_all[i]
-    bias_row = lax.broadcasted_iota(jnp.int32, rank_state.shape, 0)
-    for r in range(bias_ref.shape[0]):
-        rank_state = rank_state + jnp.where(bias_row == r, bias_ref[r], 0.0)
-    rank_state = rank_state[:, :positions]
+    grad_part = dot_nt(wq[...], all_rows(dq_rows))
 
     total = part[0]
     for k in range(1, halo + 1):
@@ -337,13 +342,15 @@
     for copy in kv_receives():
         copy.wait_recv()
     rows_kv = all_rows(kv_rows)
-    grad_part = grad_part + dot_nt(rows_kv[:, :kv_width], wk[...])
-    grad_part = grad_part + dot_nt(rows_kv[:, kv_width:], wv[...])
+    grad_part = grad_part + dot_nt(wk[...], rows_kv[:, :kv_width])
+    grad_part = grad_part + dot_nt(wv[...], rows_kv[:, kv_width:])
 
     my_slot = 2 * me + core
     if lanes > positions:
         rg_all[my_slot] = jnp.zeros(rg_all.shape[1:], F32)
-    rg_all[my_slot, :, :positions] = dot_nt(rot_ref[...], grad_part, HIGHEST)
+    rg_all[my_slot, :, :positions] = rank_up + jnp.dot(
+        rot_ref[...], grad_part, precision=HIGHEST, preferred_element_type=F32
+    )
 
     def rank_copy(i, k, flip, receive):
         slot = my_slot
@@ -360,9 +367,7 @@
         rank_copy(i, k, flip, False).start()
     if gr_own.shape[1] > width:
         gr_own[...] = jnp.zeros(gr_own.shape, F32)
-    gr_own[:, :width] = jnp.dot(
-        rank_state, grad_part, precision=HIGHEST, preferred_element_type=F32
-    )
+    gr_own[:, :width] = rot_up + dot_nt(rank_state, grad_part, HIGHEST)
     rot_copy = send(gr_own, gr_in, gr_send, gr_recv, head=1 - core)
     rot_copy.start()
     for i, (k, flip) in enumerate(pairs):
@@ -387,10 +392,24 @@
     for k in range(1, halo + 1):
         part_copy(k).wait_send()
     for j in range(1, chain + 1):
-        for p in range(2):
+        for p in range(PIECES):
             chain_copy(j, p).wait_send()
     for j in range(chain + 1):
-        exchange(j, lambda copy: copy.wait_send())
+        for p in range(PIECES):
+            exchange(j, p, lambda copy: copy.wait_send())
+
+
+def finish(rot_in, proj_in, bias_in, rot_out, proj_out, bias_out, sems):
+    copies = [
+        pltpu.make_async_copy(src, dst, sems.at[i])
+        for i, (src, dst) in enumerate(
+            ((rot_in, rot_out), (proj_in, proj_out), (bias_in, bias_out))
+        )
+    ]
+    for copy in copies:
+        copy.start()
+    for copy in copies:
+        copy.wait()
 
 
 def local(n, *args):
@@ -412,7 +431,7 @@
     smem = pl.BlockSpec(memory_space=pltpu.SMEM)
     hbm = pl.BlockSpec(memory_space=pltpu.HBM)
     dma = pltpu.SemaphoreType.DMA
-    rot, proj, bias = pl.pallas_call(
+    outs = pl.pallas_call(
         functools.partial(kernel, n),
         out_shape=(
             jax.ShapeDtypeStruct((rank, width), F32),
@@ -452,8 +471,8 @@
             pltpu.VMEM(rotation.shape, F32),
             pltpu.SMEM((rank,), F32),
             dma((len(args),)),
-            dma((chain, 2)), dma((chain, 2)),
-            dma((chain, 2)), dma((chain, 2)),
+            dma((chain, PIECES)), dma((chain, PIECES)),
+            dma((chain, PIECES)), dma((chain, PIECES)),
             dma((n,)), dma((n,)),
             dma((n,)), dma((n,)),
             dma((halo,)), dma((halo,)),
@@ -466,7 +485,14 @@
         ),
         name="rank_backward",
     )(*args)
-    return rot, proj, bias
+    return pl.pallas_call(
+        finish,
+        out_shape=tuple(jax.ShapeDtypeStruct(out.shape, out.dtype) for out in outs),
+        in_specs=[hbm] * 3,
+        out_specs=(hbm,) * 3,
+        scratch_shapes=[dma((3,))],
+        name="finish",
+    )(*outs)
 
 
 def solution(mesh):

time: 54.1 us -> 52.3 us (0.967)
  local copies, waits for them, and re-layouts: 3.79 us -> 0 us
  Pallas kernels: 49.5 us -> 51.5 us
    unnamed x3 -> x0, local copies, waits for them, and re-layouts: 3.79 us -> none
    pallas_call x0 -> x1, Pallas kernels: none -> 2.39 us  [local(): pl.pallas_call(finish, out_shape=tuple((jax.ShapeDtypeStruct(out.shape, o...]
where the time goes in v3:
time: 52.3 us; the launch traced here: 52.1 us
  Pallas kernels  51.5 us (98%)
  between operations  0.64 us (1%)
    pallas_call x1, Pallas kernels, local(): pl.pallas_call(functools.partial(kernel, n), out_shape=(jax.ShapeDtypeStr...  49.1 us
    pallas_call x1, Pallas kernels, local(): pl.pallas_call(finish, out_shape=tuple((jax.ShapeDtypeStruct(out.shape, o...  2.39 us

profile of v3, /device:TPU:0, one launch (start us, length us, event | category | flops | bytes accessed | tf_op | source)
XLA Modules:
  0.0 52.1 jit_solution(8408905156915646222)
XLA Ops:
  0.6 49.1 %rank_backward.1 = (f32[8,576]{1,0:T(8,128)}, f32[8,576]{1,0:T(8,128)}, f32[8]{0:T(128)}) custom-call(bf16[128,1024]{1,0:T(8,128)(2,1)} %q_hbm.1, bf16[128,512]{1,0:T(8,128)(2,1)} %k_hbm.1, bf16[128,512]{1,0:T(8,128)(2,1)} %v_hbm.1, bf16[128,1024]{1,0:T(8,128)(2,1)} %g_hbm.1, s32[16]{0:T(128)} %doc_hbm.1, s32[64]{0:T(128)} %pos_hbm.1, ...), custom_call_target="tpu_custom_call" | custom-call | tf_op jit(solution)/shard_map/rank_backward/pallas_call | solution.py:434
  49.7 2.4 %finish.1 = (f32[8,576]{1,0:T(8,128)}, f32[8,576]{1,0:T(8,128)}, f32[8]{0:T(128)}) custom-call(f32[8,576]{1,0:T(8,128)} %get-tuple-element.6.rot_in, f32[8,576]{1,0:T(8,128)} %get-tuple-element.7.proj_in, f32[8]{0:T(128)} %get-tuple-element.8.bias_in), custom_call_target="tpu_custom_call" | custom-call | tf_op jit(solution)/shard_map/finish/pallas_call | solution.py:488

commit v4 on v3

--- a/solution.py
+++ b/solution.py
@@ -399,17 +399,10 @@
             exchange(j, p, lambda copy: copy.wait_send())
 
 
-def finish(rot_in, proj_in, bias_in, rot_out, proj_out, bias_out, sems):
-    copies = [
-        pltpu.make_async_copy(src, dst, sems.at[i])
-        for i, (src, dst) in enumerate(
-            ((rot_in, rot_out), (proj_in, proj_out), (bias_in, bias_out))
-        )
-    ]
-    for copy in copies:
-        copy.start()
-    for copy in copies:
-        copy.wait()
+def finish(rot_in, proj_in, bias_in, rot_out, proj_out, bias_out):
+    rot_out[...] = rot_in[...]
+    proj_out[...] = proj_in[...]
+    bias_out[...] = bias_in[...]
 
 
 def local(n, *args):
@@ -488,9 +481,8 @@
     return pl.pallas_call(
         finish,
         out_shape=tuple(jax.ShapeDtypeStruct(out.shape, out.dtype) for out in outs),
-        in_specs=[hbm] * 3,
-        out_specs=(hbm,) * 3,
-        scratch_shapes=[dma((3,))],
+        in_specs=[vmem] * 3,
+        out_specs=(vmem,) * 3,
         name="finish",
     )(*outs)
 

time: 52.3 us -> 51.3 us (0.981)
  Pallas kernels: 51.5 us -> 50.5 us
    pallas_call x1, Pallas kernels: 2.39 us -> 1.36 us  [local(): pl.pallas_call(finish, out_shape=tuple((jax.ShapeDtypeStruct(out.shape, o...]
where the time goes in v4:
time: 51.3 us; the launch traced here: 51.1 us
  Pallas kernels  50.5 us (98%)
  between operations  0.64 us (1%)
    pallas_call x1, Pallas kernels, local(): pl.pallas_call(functools.partial(kernel, n), out_shape=(jax.ShapeDtypeStr...  49.1 us
    pallas_call x1, Pallas kernels, local(): pl.pallas_call(finish, out_shape=tuple((jax.ShapeDtypeStruct(out.shape, o...  1.36 us

profile of v4, /device:TPU:0, one launch (start us, length us, event | category | flops | bytes accessed | tf_op | source)
XLA Modules:
  0.0 51.1 jit_solution(155103638444409583)
XLA Ops:
  0.6 49.1 %rank_backward.1 = (f32[8,576]{1,0:T(8,128)}, f32[8,576]{1,0:T(8,128)}, f32[8]{0:T(128)}) custom-call(bf16[128,1024]{1,0:T(8,128)(2,1)} %q_hbm.1, bf16[128,512]{1,0:T(8,128)(2,1)} %k_hbm.1, bf16[128,512]{1,0:T(8,128)(2,1)} %v_hbm.1, bf16[128,1024]{1,0:T(8,128)(2,1)} %g_hbm.1, s32[16]{0:T(128)} %doc_hbm.1, s32[64]{0:T(128)} %pos_hbm.1, ...), custom_call_target="tpu_custom_call" | custom-call | tf_op jit(solution)/shard_map/rank_backward/pallas_call | solution.py:427
  49.7 1.4 %finish.1 = (f32[8,576]{1,0:T(8,128)}, f32[8,576]{1,0:T(8,128)}, f32[8]{0:T(128)}) custom-call(f32[8,576]{1,0:T(8,128)} %get-tuple-element.6.rot_in, f32[8,576]{1,0:T(8,128)} %get-tuple-element.7.proj_in, f32[8]{0:T(128)} %get-tuple-element.8.bias_in), custom_call_target="tpu_custom_call" | custom-call | tf_op jit(solution)/shard_map/finish/pallas_call | solution.py:481
